TPU v7x, 32 devices: a whole 2x2x4 slice. The times are simulated.
32 devices in a mesh: groups: 2 (over y), blk: 4 (over z), head: 4 (over x, core).
Axes of the slice: x: 2, y: 2, z: 4, core: 2. Of those that a mesh axis runs over, the one named last changes fastest.
Arguments:
- queries: bfloat16 [4, 4, 8192], P('groups', 'blk', 'head'), parts along dimension 0, may hold values from -4.5 to 4.5
- stored_cache_keys: bfloat16 [4, 2048, 1024], P('groups', 'blk', 'head'), parts along dimension 0, may hold values from -4.5 to 4.5
- stored_cache_values: bfloat16 [4, 2048, 1024], P('groups', 'blk', 'head'), parts along dimension 0, may hold values from -6 to 6
- out_weight: bfloat16 [8192, 8192], P('head', 'blk'), may hold values from -3 to 3
- lengths: int32 [4], P('groups'), parts along dimension 0, may hold values from 1024 to 2048
Outputs:
- projected: bfloat16 [4, 4, 8192], P('groups', 'head', 'blk'), parts along dimension 0
There are 2 independent parts, one for each index of `groups`. A program takes and returns all parts, laid end to end along the dimension named above; an argument that names none is the same for every part. Nothing has to cross between parts.
All inputs are finite; a program needn't handle non-finite values.
Results may differ from a plain program's by a relative error of at most 0.0056.
Values may be sent and summed in bfloat16 or wider, within the bound.
A program may use at most 64 MiB of HBM per device.

v0:
```python
import math
import jax
import jax.numpy as jnp
from jax import lax
from jax.sharding import PartitionSpec as P

REQUEST_COUNT = 2
QUERY_HEAD_COUNT = 64
KEY_VALUE_HEADS = 8
HEAD_DIMENSION = 128
masked_fill_value = -1e30


def body(queries, stored_cache_keys, stored_cache_values, out_weight, lengths):
    group_width = QUERY_HEAD_COUNT // KEY_VALUE_HEADS
    local_heads = stored_cache_keys.shape[2] // HEAD_DIMENSION
    query_heads = local_heads * group_width
    span = stored_cache_keys.shape[1]
    new_count = queries.shape[1] * lax.axis_size("blk")
    key_pos = lax.axis_index("blk") * span + jnp.arange(span, dtype=jnp.int32)
    score_scale = 1.0 / math.sqrt(HEAD_DIMENSION)
    piece = lax.all_gather(queries, "blk", axis=1, tiled=True)
    rows_count = piece.shape[1]
    query_pos = lengths[:, None] - new_count + jnp.arange(rows_count, dtype=jnp.int32)[None, :]
    sums_list = []
    maxima_list = []
    totals_list = []
    for request in range(REQUEST_COUNT):
        visible = (key_pos[None, :] <= query_pos[request][:, None])[:, None, :]
        parts_sum, parts_max, parts_total = ([], [], [])
        for kv_head in range(local_heads):
            block_query = piece[
                request,
                :,
                kv_head
                * group_width
                * HEAD_DIMENSION : (kv_head + 1)
                * group_width
                * HEAD_DIMENSION,
            ].reshape(rows_count, group_width, HEAD_DIMENSION)
            local_keys = stored_cache_keys[
                request, :, kv_head * HEAD_DIMENSION : (kv_head + 1) * HEAD_DIMENSION
            ]
            local_values = stored_cache_values[
                request, :, kv_head * HEAD_DIMENSION : (kv_head + 1) * HEAD_DIMENSION
            ]
            scores = (
                jnp.einsum(
                    "ngd,cd->ngc", block_query, local_keys, preferred_element_type=jnp.float32
                )
                * score_scale
            )
            block_max = jnp.max(jnp.where(visible, scores, masked_fill_value), axis=-1)
            weights = jnp.where(visible, jnp.exp(scores - block_max[..., None]), 0.0)
            parts_total.append(jnp.sum(weights, axis=-1))
            parts_max.append(block_max)
            weighted = jnp.einsum(
                "ngc,cd->ngd",
                weights.astype(jnp.bfloat16),
                local_values,
                preferred_element_type=jnp.float32,
            )
            parts_sum.append(weighted.reshape(rows_count, group_width * HEAD_DIMENSION))
        sums_list.append(jnp.concatenate(parts_sum, axis=1))
        maxima_list.append(jnp.concatenate(parts_max, axis=1))
        totals_list.append(jnp.concatenate(parts_total, axis=1))
    new_sums = jnp.stack(sums_list, axis=0)
    new_maxima = jnp.stack(maxima_list, axis=0)
    new_totals = jnp.stack(totals_list, axis=0)
    received = (
        lax.all_to_all(new_sums[None], "blk", split_axis=2, concat_axis=0, tiled=True),
        lax.all_to_all(new_maxima[None], "blk", split_axis=2, concat_axis=0, tiled=True),
        lax.all_to_all(new_totals[None], "blk", split_axis=2, concat_axis=0, tiled=True),
    )
    part_sums, part_max, part_totals = received
    blocks = part_sums.shape[0]
    own_rows = part_sums.shape[2]
    top = jnp.max(part_max, axis=0)
    factor = jnp.exp(part_max - top[None])
    overall = jnp.sum(factor * part_totals, axis=0)
    shaped = part_sums.reshape(blocks, REQUEST_COUNT, own_rows, query_heads, HEAD_DIMENSION)
    merged = jnp.sum(shaped * factor[..., None], axis=0) / overall[..., None]
    own_attention = merged.astype(jnp.bfloat16).reshape(
        REQUEST_COUNT, own_rows, query_heads * HEAD_DIMENSION
    )
    terms = jnp.einsum(
        "rnc,cd->rnd",
        lax.all_gather(own_attention, "blk", axis=1, tiled=True),
        out_weight,
        preferred_element_type=jnp.float32,
    )
    return lax.psum_scatter(terms, "head", scatter_dimension=1, tiled=True).astype(jnp.bfloat16)


def solution(mesh):
    placed = (
        P("groups", "blk", "head"),
        P("groups", "blk", "head"),
        P("groups", "blk", "head"),
        P("head", "blk"),
        P("groups"),
    )
    return jax.shard_map(
        body, mesh=mesh, in_specs=placed, out_specs=P("groups", "head", "blk"), check_vma=False
    )
```

profile of v0, /device:TPU:0, one launch (start us, length us, event | category | flops | bytes accessed | tf_op | source)
XLA Modules:
  0.0 82.9 jit_solution(6853491526789684254)
XLA Ops:
  0.0 0.7 broadcast_add_fusion
  0.7 15.0 %all_gather.6 = bf16[2,4,2048]{2,0,1:T(2,128)(2,1)S(1)} all-gather(bf16[2,1,2048]{2,0,1:T(2,128)(2,1)} %param.5), channel_id=1, replica_groups=mesh['groups'=2,'blk'=4,'head'=4] {'blk'}, dimensions={1}, use_global_device_ids=true | all-gather | bytes 40960 | tf_op jit(solution)/shard_map/all_gather | solution.py:22
  16.0 1.1 %select_reduce_fusion.3 = (f32[4,8]{1,0:T(4,128)S(1)}, f32[4,8,512]{2,1,0:T(8,128)S(1)}) fusion(pred[4,512]{1,0:T(4,128)(4,1)S(1)} %get-tuple-element.13, bf16[2,512,256]{2,1,0:T(8,128)(2,1)} %param.6, bf16[1,4,8,128]{3,1,2,0:T(4,128)(2,1)S(1)} %bitcast.152), kind=kOutput, calls=%fused_computation.36 | convolution fusion | flops 4243424 | bytes 206976 | tf_op jit(solution)/shard_map/ngd,cd->ngc/dot_general | solution.py:48
  17.2 1.1 %select_reduce_fusion.1 = (f32[4,8]{1,0:T(4,128)S(1)}, f32[4,8,512]{2,1,0:T(8,128)S(1)}) fusion(pred[4,512]{1,0:T(4,128)(4,1)S(1)} %get-tuple-element.14, bf16[2,512,256]{2,1,0:T(8,128)(2,1)} %param.6, bf16[1,4,8,128]{3,1,2,0:T(4,128)(2,1)S(1)} %bitcast.151), kind=kOutput, calls=%fused_computation.32 | convolution fusion | flops 4243424 | bytes 206976 | tf_op jit(solution)/shard_map/ngd,cd->ngc/dot_general | solution.py:48
  18.3 1.1 %fusion.19 = (f32[4,8]{1,0:T(4,128)S(1)}, f32[4,8]{1,0:T(4,128)S(1)}, f32[4,8,512]{2,1,0:T(8,128)S(1)}) fusion(f32[4,8,512]{2,1,0:T(8,128)S(1)} %get-tuple-element.21, f32[4,8]{1,0:T(4,128)S(1)} %get-tuple-element.20, pred[4,512]{1,0:T(4,128)(4,1)S(1)} %get-tuple-element.13, bf16[2,512,256]{2,1,0:T(8,128)(2,1)} %param.6, ...), kind=kOutput, calls=%fused_computation.37 | convolution fusion | flops 4292544 | bytes 272768 | tf_op jit(solution)/shard_map/ngd,cd->ngc/dot_general | solution.py:48
  19.4 1.1 %fusion.23 = (f32[4,8]{1,0:T(4,128)S(1)}, f32[4,8]{1,0:T(4,128)S(1)}, f32[4,8,512]{2,1,0:T(8,128)S(1)}) fusion(f32[4,8,512]{2,1,0:T(8,128)S(1)} %get-tuple-element.18, f32[4,8]{1,0:T(4,128)S(1)} %get-tuple-element.17, pred[4,512]{1,0:T(4,128)(4,1)S(1)} %get-tuple-element.14, bf16[2,512,256]{2,1,0:T(8,128)(2,1)} %param.6, ...), kind=kOutput, calls=%fused_computation.41 | convolution fusion | flops 4292544 | bytes 272768 | tf_op jit(solution)/shard_map/ngd,cd->ngc/dot_general | solution.py:48
  20.7 0.6 copy.16
  21.3 4.6 %all-to-all-start.1 = ((f32[1,2,4,16]{3,1,0,2:T(2,128)}), f32[1,2,4,16]{3,1,0,2:T(2,128)S(1)}, u32[]{:S(2)}, u32[]{:S(2)}) async-start(f32[1,2,4,16]{3,1,0,2:T(2,128)} %copy.16), calls=%async_computation.1 | async-start | bytes 8192 | tf_op jit(solution)/shard_map/all_to_all | solution.py:72
  25.9 1.1 %convolution_bitcast_fusion.3 = f32[1,4,8,128]{3,2,1,0:T(8,128)S(1)} fusion(bf16[2,512,256]{2,1,0:T(8,128)(2,1)} %param.7, f32[4,8,512]{2,1,0:T(8,128)S(1)} %get-tuple-element.21, f32[4,8]{1,0:T(4,128)S(1)} %get-tuple-element.20, pred[4,512]{1,0:T(4,128)(4,1)S(1)} %get-tuple-element.13), kind=kOutput, calls=%fused_computation.9 | convolution fusion | flops 4243456 | bytes 215168 | tf_op jit(solution)/shard_map/ngc,cd->ngd/dot_general | solution.py:57
  27.0 1.1 %convolution_bitcast_fusion.1 = f32[1,4,8,128]{3,2,1,0:T(8,128)S(1)} fusion(bf16[2,512,256]{2,1,0:T(8,128)(2,1)} %param.7, f32[4,8,512]{2,1,0:T(8,128)S(1)} %get-tuple-element.18, f32[4,8]{1,0:T(4,128)S(1)} %get-tuple-element.17, pred[4,512]{1,0:T(4,128)(4,1)S(1)} %get-tuple-element.14), kind=kOutput, calls=%fused_computation.7 | convolution fusion | flops 4243456 | bytes 215168 | tf_op jit(solution)/shard_map/ngc,cd->ngd/dot_general | solution.py:57
  28.1 1.1 %convolution_bitcast_fusion.2 = f32[1,4,8,128]{3,2,1,0:T(8,128)S(1)} fusion(bf16[2,512,256]{2,1,0:T(8,128)(2,1)} %param.7, f32[4,8,512]{2,1,0:T(8,128)S(1)} %get-tuple-element.22, f32[4,8]{1,0:T(4,128)S(1)} %get-tuple-element.10, pred[4,512]{1,0:T(4,128)(4,1)S(1)} %get-tuple-element.13), kind=kOutput, calls=%fused_computation.8 | convolution fusion | flops 4243456 | bytes 215168 | tf_op jit(solution)/shard_map/ngc,cd->ngd/dot_general | solution.py:57
  29.2 0.2 fusion.21
  29.4 1.1 %convolution_bitcast_fusion = f32[1,4,8,128]{3,2,1,0:T(8,128)S(1)} fusion(bf16[2,512,256]{2,1,0:T(8,128)(2,1)} %param.7, f32[4,8,512]{2,1,0:T(8,128)S(1)} %get-tuple-element.19, f32[4,8]{1,0:T(4,128)S(1)} %get-tuple-element.12, pred[4,512]{1,0:T(4,128)(4,1)S(1)} %get-tuple-element.14), kind=kOutput, calls=%fused_computation.6 | convolution fusion | flops 4243456 | bytes 215168 | tf_op jit(solution)/shard_map/ngc,cd->ngd/dot_general | solution.py:57
  30.8 0.7 maximum_bitcast_fusion
  31.5 0.6 copy.20
  32.1 1.2 %dynamic-slice = u32[1]{0:T(128)} dynamic-slice(u32[32]{0:T(128)} %constant.21, u32[]{:T(128)S(6)} %add.33), dynamic_slice_sizes={1} | dynamic-slice | bytes 12
  33.4 5.1 %all-to-all-start.2 = ((f32[1,2,4,16]{3,1,0,2:T(2,128)}), f32[1,2,4,16]{3,1,0,2:T(2,128)S(1)}, u32[]{:S(2)}, u32[]{:S(2)}) async-start(f32[1,2,4,16]{3,1,0,2:T(2,128)} %copy.20), calls=%async_computation.2 | async-start | bytes 8192 | tf_op jit(solution)/shard_map/all_to_all | solution.py:73
  38.5 5.5 %all-to-all-done.2 = f32[1,2,4,16]{3,1,0,2:T(2,128)S(1)} async-done(((f32[1,2,4,16]{3,1,0,2:T(2,128)}), f32[1,2,4,16]{3,1,0,2:T(2,128)S(1)}, u32[]{:S(2)}, u32[]{:S(2)}) %all-to-all-start.2) | async-done | bytes 544 | tf_op jit(solution)/shard_map/all_to_all | solution.py:73
  44.0 3.3 %all-to-all-start = ((f32[1,2,4,2048]{3,1,0,2:T(2,128)}), f32[1,2,4,2048]{3,1,0,2:T(2,128)S(1)}, u32[]{:S(2)}, u32[]{:S(2)}) async-start(f32[1,2,4,2048]{3,1,0,2:T(2,128)} %maximum_bitcast_fusion), calls=%async_computation | async-start | bytes 131072 | tf_op jit(solution)/shard_map/all_to_all | solution.py:71
  47.6 5.5 %all-to-all-done = f32[1,2,4,2048]{3,1,0,2:T(2,128)S(1)} async-done(((f32[1,2,4,2048]{3,1,0,2:T(2,128)}), f32[1,2,4,2048]{3,1,0,2:T(2,128)S(1)}, u32[]{:S(2)}, u32[]{:S(2)}) %all-to-all-start) | async-done | bytes 65568 | tf_op jit(solution)/shard_map/all_to_all | solution.py:71
  53.1 13.1 %all_gather.7 = bf16[2,4,2048]{2,0,1:T(2,128)(2,1)S(1)} all-gather(bf16[2,1,2048]{2,0,1:T(2,128)(2,1)S(1)} %fusion.43), channel_id=1, replica_groups=mesh['groups'=2,'blk'=4,'head'=4] {'blk'}, dimensions={1}, use_global_device_ids=true | all-gather | bytes 40960 | tf_op jit(solution)/shard_map/all_gather | solution.py:88
  66.2 4.7 %fusion = f32[2,4,2048]{2,0,1:T(2,128)S(1)} fusion(bf16[2,4,2048]{2,0,1:T(2,128)(2,1)S(1)} %all_gather.7, bf16[2048,2048]{1,0:T(8,128)(2,1)} %param.8), kind=kOutput, calls=%fused_computation | convolution fusion | flops 67108864 | bytes 8486912 | tf_op jit(solution)/shard_map/rnc,cd->rnd/dot_general | solution.py:86
  71.0 10.7 %all-reduce = bf16[2,4,2048]{2,0,1:T(2,128)(2,1)S(1)} all-reduce(f32[2,4,2048]{2,0,1:T(2,128)S(1)} %fusion), channel_id=2, replica_groups=mesh['groups'=2,'blk'=4,'head'=4] {'head'}, use_global_device_ids=true, to_apply=%region_11.12.clone | all-reduce | flops 16384 | bytes 98304
  81.6 1.2 %dynamic-slice_convert_fusion = bf16[2,1,2048]{2,0,1:T(2,128)(2,1)} fusion(bf16[2,4,2048]{2,0,1:T(2,128)(2,1)S(1)} %all-reduce, u32[]{:T(128)} %bitcast.39), kind=kLoop, calls=%fused_computation.67 | loop fusion | bytes 16388 | tf_op jit(solution)/shard_map/convert_element_type | solution.py:92
  (30 shorter events, 1.0 us)
Async XLA Ops:
  21.3 12.1 %all-to-all-start.1 = ((f32[1,2,4,16]{3,1,0,2:T(2,128)}), f32[1,2,4,16]{3,1,0,2:T(2,128)S(1)}, u32[]{:S(2)}, u32[]{:S(2)}) async-start(f32[1,2,4,16]{3,1,0,2:T(2,128)} %copy.16), calls=%async_computation.1 | async-start | bytes 8192 | tf_op jit(solution)/shard_map/all_to_all | solution.py:72
  33.4 10.7 %all-to-all-start.2 = ((f32[1,2,4,16]{3,1,0,2:T(2,128)}), f32[1,2,4,16]{3,1,0,2:T(2,128)S(1)}, u32[]{:S(2)}, u32[]{:S(2)}) async-start(f32[1,2,4,16]{3,1,0,2:T(2,128)} %copy.20), calls=%async_computation.2 | async-start | bytes 8192 | tf_op jit(solution)/shard_map/all_to_all | solution.py:73
  44.0 9.0 %all-to-all-start = ((f32[1,2,4,2048]{3,1,0,2:T(2,128)}), f32[1,2,4,2048]{3,1,0,2:T(2,128)S(1)}, u32[]{:S(2)}, u32[]{:S(2)}) async-start(f32[1,2,4,2048]{3,1,0,2:T(2,128)} %maximum_bitcast_fusion), calls=%async_computation | async-start | bytes 131072 | tf_op jit(solution)/shard_map/all_to_all | solution.py:71
where the time goes:
time: 83.4 us; the launch traced here: 82.9 us
  blocking collectives  38.8 us (47%)
  matrix products  13.7 us (16%)
  starting transfers between devices  13 us (16%)
  waiting for transfers between devices  11 us (13%)
  local copies, waits for them, and re-layouts  4.11 us (5%)
  other arithmetic  2.04 us (2%)
    all_gather x1, blocking collectives, body(): piece = lax.all_gather(queries, 'blk', axis=1, tiled=True)  15 us
    all_gather x1, blocking collectives, body(): lax.all_gather(own_attention, 'blk', axis=1, tiled=True)  13.1 us
    unnamed x1, blocking collectives  10.7 us
    all_to_all x1, waiting for transfers between devices, body(): lax.all_to_all(new_totals[None], 'blk', split_axis=2, concat_axis=0, tile...  5.54 us
    all_to_all x1, waiting for transfers between devices, body(): lax.all_to_all(new_sums[None], 'blk', split_axis=2, concat_axis=0, tiled=...  5.46 us
    all_to_all x1, starting transfers between devices, body(): lax.all_to_all(new_totals[None], 'blk', split_axis=2, concat_axis=0, tile...  5.09 us
    dot_general x1, matrix products, body(): jnp.einsum('rnc,cd->rnd', lax.all_gather(own_attention, 'blk', axis=1, ti...  4.71 us
    all_to_all x1, starting transfers between devices, body(): lax.all_to_all(new_maxima[None], 'blk', split_axis=2, concat_axis=0, tile...  4.63 us
  transfers between devices with their start and end apart: 3, of which 2 were waited for; matrix products, arithmetic and copies ran while one was open for 9% of the time, Pallas kernels for 0%

commit v1 on v0

--- a/solution.py
+++ b/solution.py
@@ -9,6 +9,21 @@
 KEY_VALUE_HEADS = 8
 HEAD_DIMENSION = 128
 masked_fill_value = -1e30
+
+
+def on_each_block(array, axis, dim, make, out_dim):
+    ways, here, hop = (lax.axis_size(axis), lax.axis_index(axis), array.shape[dim])
+    results = []
+    for far in range(ways):
+        arriving = (
+            lax.ppermute(array, axis, [(d, (d + 1) % ways) for d in range(ways)])
+            if far + 1 < ways
+            else array
+        )
+        results.append(make(array, (here - far) % ways * hop))
+        array = arriving
+    line = jnp.concatenate(results[::-1], axis=out_dim)
+    return jnp.roll(line, (here + 1) * results[0].shape[out_dim], axis=out_dim)
 
 
 def body(queries, stored_cache_keys, stored_cache_values, out_weight, lengths):
@@ -83,11 +98,14 @@
     own_attention = merged.astype(jnp.bfloat16).reshape(
         REQUEST_COUNT, own_rows, query_heads * HEAD_DIMENSION
     )
-    terms = jnp.einsum(
-        "rnc,cd->rnd",
-        lax.all_gather(own_attention, "blk", axis=1, tiled=True),
-        out_weight,
-        preferred_element_type=jnp.float32,
+    terms = on_each_block(
+        own_attention,
+        "blk",
+        1,
+        lambda shard, offset: jnp.einsum(
+            "rnc,cd->rnd", shard, out_weight, preferred_element_type=jnp.float32
+        ),
+        1,
     )
     return lax.psum_scatter(terms, "head", scatter_dimension=1, tiled=True).astype(jnp.bfloat16)
 

time: 83.4 us -> 93.7 us (1.12)
  waiting for transfers between devices: 11 us -> 25 us
  blocking collectives: 38.8 us -> 25.7 us
  matrix products: 13.7 us -> 20.7 us
  local copies, waits for them, and re-layouts: 4.11 us -> 5.49 us
  starting transfers between devices: 13 us -> 14 us
    ppermute x0 -> x3, waiting for transfers between devices: none -> 14 us  [on_each_block(): lax.ppermute(array, axis, [(d, (d + 1) % ways) for d in range(ways)])]
    all_gather x1 -> x0, blocking collectives: 13.1 us -> none  [body(): lax.all_gather(own_attention, 'blk', axis=1, tiled=True)]
    dot_general x1 -> x4, matrix products: 4.71 us -> 11.7 us  [body(): jnp.einsum('rnc,cd->rnd', shard, out_weight, preferred_element_type=jnp.f...]
    unnamed x5 -> x13, local copies, waits for them, and re-layouts: 1.27 us -> 2.55 us
    ppermute x0 -> x3, starting transfers between devices: none -> 0.97 us  [on_each_block(): lax.ppermute(array, axis, [(d, (d + 1) % ways) for d in range(ways)])]
  transfers between devices with their start and end apart: 3 -> 6, of which waited for: 2 -> 5; matrix products, arithmetic and copies ran while one was open for 9% -> 8% of each run, Pallas kernels for 0% -> 0%
where the time goes in v1:
time: 93.7 us; the launch traced here: 93.1 us
  blocking collectives  25.7 us (27%)
  waiting for transfers between devices  25 us (27%)
  matrix products  20.7 us (22%)
  starting transfers between devices  14 us (15%)
  local copies, waits for them, and re-layouts  5.49 us (6%)
  other arithmetic  2.05 us (2%)
    all_gather x1, blocking collectives, body(): piece = lax.all_gather(queries, 'blk', axis=1, tiled=True)  15 us
    ppermute x3, waiting for transfers between devices, on_each_block(): lax.ppermute(array, axis, [(d, (d + 1) % ways) for d in range(ways)])  14 us
    dot_general x4, matrix products, body(): jnp.einsum('rnc,cd->rnd', shard, out_weight, preferred_element_type=jnp.f...  11.7 us
    unnamed x1, blocking collectives  10.7 us
    all_to_all x1, waiting for transfers between devices, body(): lax.all_to_all(new_sums[None], 'blk', split_axis=2, concat_axis=0, tiled=...  5.59 us
    all_to_all x1, waiting for transfers between devices, body(): lax.all_to_all(new_totals[None], 'blk', split_axis=2, concat_axis=0, tile...  5.42 us
    all_to_all x1, starting transfers between devices, body(): lax.all_to_all(new_totals[None], 'blk', split_axis=2, concat_axis=0, tile...  5.09 us
    all_to_all x1, starting transfers between devices, body(): lax.all_to_all(new_maxima[None], 'blk', split_axis=2, concat_axis=0, tile...  4.63 us
  transfers between devices with their start and end apart: 6, of which 5 were waited for; matrix products, arithmetic and copies ran while one was open for 8% of the time, Pallas kernels for 0%

profile of v1, /device:TPU:0, one launch (start us, length us, event | category | flops | bytes accessed | tf_op | source)
XLA Modules:
  0.0 93.1 jit_solution(7944270323710368135)
XLA Ops:
  0.7 15.0 %all_gather.3 = bf16[2,4,2048]{2,0,1:T(2,128)(2,1)S(1)} all-gather(bf16[2,1,2048]{2,0,1:T(2,128)(2,1)} %param.5), channel_id=1, replica_groups=mesh['groups'=2,'blk'=4,'head'=4] {'blk'}, dimensions={1}, use_global_device_ids=true | all-gather | bytes 40960 | tf_op jit(solution)/shard_map/all_gather | solution.py:37
  16.0 1.1 %select_reduce_fusion.3 = (f32[4,8]{1,0:T(4,128)S(1)}, f32[4,8,512]{2,1,0:T(8,128)S(1)}) fusion(pred[4,512]{1,0:T(4,128)(4,1)S(1)} %get-tuple-element.13, bf16[2,512,256]{2,1,0:T(8,128)(2,1)} %param.6, bf16[1,4,8,128]{3,1,2,0:T(4,128)(2,1)S(1)} %bitcast.186), kind=kOutput, calls=%fused_computation.38 | convolution fusion | flops 4243424 | bytes 206976 | tf_op jit(solution)/shard_map/ngd,cd->ngc/dot_general | solution.py:63
  17.2 1.1 %select_reduce_fusion.1 = (f32[4,8]{1,0:T(4,128)S(1)}, f32[4,8,512]{2,1,0:T(8,128)S(1)}) fusion(pred[4,512]{1,0:T(4,128)(4,1)S(1)} %get-tuple-element.14, bf16[2,512,256]{2,1,0:T(8,128)(2,1)} %param.6, bf16[1,4,8,128]{3,1,2,0:T(4,128)(2,1)S(1)} %bitcast.185), kind=kOutput, calls=%fused_computation.34 | convolution fusion | flops 4243424 | bytes 206976 | tf_op jit(solution)/shard_map/ngd,cd->ngc/dot_general | solution.py:63
  18.3 1.1 %fusion.17 = (f32[4,8]{1,0:T(4,128)S(1)}, f32[4,8]{1,0:T(4,128)S(1)}, f32[4,8,512]{2,1,0:T(8,128)S(1)}) fusion(f32[4,8,512]{2,1,0:T(8,128)S(1)} %get-tuple-element.21, f32[4,8]{1,0:T(4,128)S(1)} %get-tuple-element.20, pred[4,512]{1,0:T(4,128)(4,1)S(1)} %get-tuple-element.13, bf16[2,512,256]{2,1,0:T(8,128)(2,1)} %param.6, ...), kind=kOutput, calls=%fused_computation.39 | convolution fusion | flops 4292544 | bytes 272768 | tf_op jit(solution)/shard_map/ngd,cd->ngc/dot_general | solution.py:63
  19.4 1.1 %fusion.21 = (f32[4,8]{1,0:T(4,128)S(1)}, f32[4,8]{1,0:T(4,128)S(1)}, f32[4,8,512]{2,1,0:T(8,128)S(1)}) fusion(f32[4,8,512]{2,1,0:T(8,128)S(1)} %get-tuple-element.18, f32[4,8]{1,0:T(4,128)S(1)} %get-tuple-element.17, pred[4,512]{1,0:T(4,128)(4,1)S(1)} %get-tuple-element.14, bf16[2,512,256]{2,1,0:T(8,128)(2,1)} %param.6, ...), kind=kOutput, calls=%fused_computation.43 | convolution fusion | flops 4292544 | bytes 272768 | tf_op jit(solution)/shard_map/ngd,cd->ngc/dot_general | solution.py:63
  21.3 4.6 %all-to-all-start.1 = ((f32[1,2,4,16]{3,1,0,2:T(2,128)}), f32[1,2,4,16]{3,1,0,2:T(2,128)S(1)}, u32[]{:S(2)}, u32[]{:S(2)}) async-start(f32[1,2,4,16]{3,1,0,2:T(2,128)} %copy.14), calls=%async_computation.1 | async-start | bytes 8192 | tf_op jit(solution)/shard_map/all_to_all | solution.py:87
  27.0 1.1 %convolution_bitcast_fusion.5 = f32[1,4,8,128]{3,2,1,0:T(8,128)S(1)} fusion(bf16[2,512,256]{2,1,0:T(8,128)(2,1)} %param.7, f32[4,8,512]{2,1,0:T(8,128)S(1)} %get-tuple-element.18, f32[4,8]{1,0:T(4,128)S(1)} %get-tuple-element.17, pred[4,512]{1,0:T(4,128)(4,1)S(1)} %get-tuple-element.14), kind=kOutput, calls=%fused_computation.9 | convolution fusion | flops 4243456 | bytes 215168 | tf_op jit(solution)/shard_map/ngc,cd->ngd/dot_general | solution.py:72
  28.1 1.1 %convolution_bitcast_fusion.6 = f32[1,4,8,128]{3,2,1,0:T(8,128)S(1)} fusion(bf16[2,512,256]{2,1,0:T(8,128)(2,1)} %param.7, f32[4,8,512]{2,1,0:T(8,128)S(1)} %get-tuple-element.22, f32[4,8]{1,0:T(4,128)S(1)} %get-tuple-element.10, pred[4,512]{1,0:T(4,128)(4,1)S(1)} %get-tuple-element.13), kind=kOutput, calls=%fused_computation.10 | convolution fusion | flops 4243456 | bytes 215168 | tf_op jit(solution)/shard_map/ngc,cd->ngd/dot_general | solution.py:72
  29.2 1.1 %convolution_bitcast_fusion.4 = f32[1,4,8,128]{3,2,1,0:T(8,128)S(1)} fusion(bf16[2,512,256]{2,1,0:T(8,128)(2,1)} %param.7, f32[4,8,512]{2,1,0:T(8,128)S(1)} %get-tuple-element.19, f32[4,8]{1,0:T(4,128)S(1)} %get-tuple-element.12, pred[4,512]{1,0:T(4,128)(4,1)S(1)} %get-tuple-element.14), kind=kOutput, calls=%fused_computation.8 | convolution fusion | flops 4243456 | bytes 215168 | tf_op jit(solution)/shard_map/ngc,cd->ngd/dot_general | solution.py:72
  32.1 5.1 %all-to-all-start.2 = ((f32[1,2,4,16]{3,1,0,2:T(2,128)}), f32[1,2,4,16]{3,1,0,2:T(2,128)S(1)}, u32[]{:S(2)}, u32[]{:S(2)}) async-start(f32[1,2,4,16]{3,1,0,2:T(2,128)} %copy.18), calls=%async_computation.2 | async-start | bytes 8192 | tf_op jit(solution)/shard_map/all_to_all | solution.py:88
  37.4 5.4 %all-to-all-done.2 = f32[1,2,4,16]{3,1,0,2:T(2,128)S(1)} async-done(((f32[1,2,4,16]{3,1,0,2:T(2,128)}), f32[1,2,4,16]{3,1,0,2:T(2,128)S(1)}, u32[]{:S(2)}, u32[]{:S(2)}) %all-to-all-start.2) | async-done | bytes 544 | tf_op jit(solution)/shard_map/all_to_all | solution.py:88
  42.8 3.3 %all-to-all-start = ((f32[1,2,4,2048]{3,1,0,2:T(2,128)}), f32[1,2,4,2048]{3,1,0,2:T(2,128)S(1)}, u32[]{:S(2)}, u32[]{:S(2)}) async-start(f32[1,2,4,2048]{3,1,0,2:T(2,128)} %maximum_bitcast_fusion), calls=%async_computation | async-start | bytes 131072 | tf_op jit(solution)/shard_map/all_to_all | solution.py:86
  46.2 5.6 %all-to-all-done = f32[1,2,4,2048]{3,1,0,2:T(2,128)S(1)} async-done(((f32[1,2,4,2048]{3,1,0,2:T(2,128)}), f32[1,2,4,2048]{3,1,0,2:T(2,128)S(1)}, u32[]{:S(2)}, u32[]{:S(2)}) %all-to-all-start) | async-done | bytes 65568 | tf_op jit(solution)/shard_map/all_to_all | solution.py:86
  52.8 4.5 %collective-permute-done = bf16[2,1,2048]{2,0,1:T(2,128)(2,1)S(1)} collective-permute-done((bf16[2,1,2048]{2,0,1:T(2,128)(2,1)S(1)}, bf16[2,1,2048]{2,0,1:T(2,128)(2,1)S(1)}, u32[]{:S(2)}, u32[]{:S(2)}) %collective-permute-start) | collective-permute-done | bytes 8224 | tf_op jit(solution)/shard_map/ppermute | solution.py:19
  57.4 1.3 %dynamic-slice = u32[1]{0:T(128)} dynamic-slice(u32[32]{0:T(128)} %constant.45, u32[]{:T(128)S(6)} %add.49), dynamic_slice_sizes={1} | dynamic-slice | bytes 12
  58.7 4.1 %collective-permute-done.1 = bf16[2,1,2048]{2,0,1:T(2,128)(2,1)S(1)} collective-permute-done((bf16[2,1,2048]{2,0,1:T(2,128)(2,1)S(1)}, bf16[2,1,2048]{2,0,1:T(2,128)(2,1)S(1)}, u32[]{:S(2)}, u32[]{:S(2)}) %collective-permute-start.1) | collective-permute-done | bytes 8224 | tf_op jit(solution)/shard_map/ppermute | solution.py:19
  62.9 5.4 %collective-permute-done.2 = bf16[2,1,2048]{2,0,1:T(2,128)(2,1)S(1)} collective-permute-done((bf16[2,1,2048]{2,0,1:T(2,128)(2,1)S(1)}, bf16[2,1,2048]{2,0,1:T(2,128)(2,1)S(1)}, u32[]{:S(2)}, u32[]{:S(2)}) %collective-permute-start.2) | collective-permute-done | bytes 8224 | tf_op jit(solution)/shard_map/ppermute | solution.py:19
  68.3 4.6 %constant_dynamic-update-slice_fusion.7 = (f32[2,8,2048]{2,0,1:T(2,128)S(1)}, f32[2,1,2048]{2,0,1:T(2,128)S(1)}) fusion(bf16[2048,2048]{1,0:T(8,128)(2,1)} %param.8, bf16[2,1,2048]{2,0,1:T(2,128)(2,1)S(1)} %collective-permute-done.2), kind=kOutput, calls=%fused_computation.68 | convolution fusion | flops 16777215 | bytes 8429568 | tf_op jit(solution)/shard_map/rnc,cd->rnd/dot_general | solution.py:105
  72.8 4.7 %constant_dynamic-update-slice_fusion.6 = (f32[2,8,2048]{2,0,1:T(2,128)S(1)}, f32[2,1,2048]{2,0,1:T(2,128)S(1)}) fusion(f32[2,8,2048]{2,0,1:T(2,128)S(1)} %get-tuple-element.23, bf16[2048,2048]{1,0:T(8,128)(2,1)} %param.8, bf16[2,1,2048]{2,0,1:T(2,128)(2,1)S(1)} %collective-permute-done.1), kind=kOutput, calls=%fused_computation.67 | convolution fusion | flops 16777216 | bytes 8429568 | tf_op jit(solution)/shard_map/rnc,cd->rnd/dot_general | solution.py:105
  77.6 1.1 %slice-done.1 = s8[4194304]{0:T(1024)(128)(4,1)S(1)} async-done(((s8[8388608]{0:T(1024)(128)(4,1)}), s8[4194304]{0:T(1024)(128)(4,1)S(1)}, s32[]{:S(2)}) %slice-start.1) | async-done | bytes 4194328
  78.7 1.2 %constant_dynamic-update-slice_fusion.5 = (f32[2,8,2048]{2,0,1:T(2,128)S(1)}, f32[2,1,2048]{2,0,1:T(2,128)S(1)}) fusion(f32[2,8,2048]{2,0,1:T(2,128)S(1)} %get-tuple-element.25, bf16[2048,2048]{1,0:T(8,128)(2,1)S(1)} %bitcast.178, bf16[2,1,2048]{2,0,1:T(2,128)(2,1)S(1)} %collective-permute-done), kind=kOutput, calls=%fused_computation.66 | convolution fusion | flops 16777216 | bytes 8429568 | tf_op jit(solution)/shard_map/rnc,cd->rnd/dot_general | solution.py:105
  79.9 1.2 %constant_dynamic-update-slice_fusion.4 = (f32[2,8,2048]{2,0,1:T(2,128)S(1)}, f32[2,1,2048]{2,0,1:T(2,128)S(1)}) fusion(f32[2,8,2048]{2,0,1:T(2,128)S(1)} %get-tuple-element.27, bf16[2048,2048]{1,0:T(8,128)(2,1)S(1)} %bitcast.178, f32[2,2048]{1,0:T(2,128)S(1)} %fusion.16, f32[1,2,16,128]{3,2,1,0:T(8,128)S(1)} %broadcast_bitcast_fusion), kind=kOutput, calls=%fused_computation.65 | convolution fusion | flops 16785408 | bytes 8454144 | tf_op jit(solution)/shard_map/rnc,cd->rnd/dot_general | solution.py:105
  81.2 10.7 %all-reduce = bf16[2,4,2048]{2,0,1:T(2,128)(2,1)S(1)} all-reduce(f32[2,4,2048]{2,0,1:T(2,128)S(1)} %constant_dynamic-slice_fusion), channel_id=2, replica_groups=mesh['groups'=2,'blk'=4,'head'=4] {'head'}, use_global_device_ids=true, to_apply=%region_11.12.clone | all-reduce | flops 16384 | bytes 98304
  91.8 1.3 %dynamic-slice_convert_fusion = bf16[2,1,2048]{2,0,1:T(2,128)(2,1)} fusion(bf16[2,4,2048]{2,0,1:T(2,128)(2,1)S(1)} %all-reduce, u32[]{:T(128)} %bitcast.45), kind=kLoop, calls=%fused_computation.78 | loop fusion | bytes 16388 | tf_op jit(solution)/shard_map/convert_element_type | solution.py:110
  (49 shorter events, 5.9 us)
Async XLA Ops:
  21.3 10.8 %all-to-all-start.1 = ((f32[1,2,4,16]{3,1,0,2:T(2,128)}), f32[1,2,4,16]{3,1,0,2:T(2,128)S(1)}, u32[]{:S(2)}, u32[]{:S(2)}) async-start(f32[1,2,4,16]{3,1,0,2:T(2,128)} %copy.14), calls=%async_computation.1 | async-start | bytes 8192 | tf_op jit(solution)/shard_map/all_to_all | solution.py:87
  32.1 10.7 %all-to-all-start.2 = ((f32[1,2,4,16]{3,1,0,2:T(2,128)}), f32[1,2,4,16]{3,1,0,2:T(2,128)S(1)}, u32[]{:S(2)}, u32[]{:S(2)}) async-start(f32[1,2,4,16]{3,1,0,2:T(2,128)} %copy.18), calls=%async_computation.2 | async-start | bytes 8192 | tf_op jit(solution)/shard_map/all_to_all | solution.py:88
  42.8 9.0 %all-to-all-start = ((f32[1,2,4,2048]{3,1,0,2:T(2,128)}), f32[1,2,4,2048]{3,1,0,2:T(2,128)S(1)}, u32[]{:S(2)}, u32[]{:S(2)}) async-start(f32[1,2,4,2048]{3,1,0,2:T(2,128)} %maximum_bitcast_fusion), calls=%async_computation | async-start | bytes 131072 | tf_op jit(solution)/shard_map/all_to_all | solution.py:86
  51.9 5.5 %collective-permute-start = (bf16[2,1,2048]{2,0,1:T(2,128)(2,1)S(1)}, bf16[2,1,2048]{2,0,1:T(2,128)(2,1)S(1)}, u32[]{:S(2)}, u32[]{:S(2)}) collective-permute-start(bf16[2,1,2048]{2,0,1:T(2,128)(2,1)S(1)} %fusion.41), channel_id=1, source_target_pairs={{0,4},{4,8},{8,12},{12,0},{1,5},{5,9},{9,13},{13,1},{2,6},{6,10},{... | collective-permute-start | bytes 24584 | tf_op jit(solution)/shard_map/ppermute | solution.py:19
  57.4 5.4 %collective-permute-start.1 = (bf16[2,1,2048]{2,0,1:T(2,128)(2,1)S(1)}, bf16[2,1,2048]{2,0,1:T(2,128)(2,1)S(1)}, u32[]{:S(2)}, u32[]{:S(2)}) collective-permute-start(bf16[2,1,2048]{2,0,1:T(2,128)(2,1)S(1)} %collective-permute-done), channel_id=1, source_target_pairs={{0,4},{4,8},{8,12},{12,0},{1,5},{5,9},{9,13},{13,1},{2,6},{6,10},{... | collective-permute-start | bytes 24584 | tf_op jit(solution)/shard_map/ppermute | solution.py:19
  62.8 5.4 %collective-permute-start.2 = (bf16[2,1,2048]{2,0,1:T(2,128)(2,1)S(1)}, bf16[2,1,2048]{2,0,1:T(2,128)(2,1)S(1)}, u32[]{:S(2)}, u32[]{:S(2)}) collective-permute-start(bf16[2,1,2048]{2,0,1:T(2,128)(2,1)S(1)} %collective-permute-done.1), channel_id=1, source_target_pairs={{0,4},{4,8},{8,12},{12,0},{1,5},{5,9},{9,13},{13,1},{2,6},{6,10},{... | collective-permute-start | bytes 24584 | tf_op jit(solution)/shard_map/ppermute | solution.py:19
  72.8 4.7 %slice-start = ((s8[8388608]{0:T(1024)(128)(4,1)}), s8[4194304]{0:T(1024)(128)(4,1)S(1)}, s32[]{:S(2)}) async-start(s8[8388608]{0:T(1024)(128)(4,1)} %bitcast.177), calls=%async_computation.3 | async-start | bytes 8388608
  72.8 5.9 %slice-start.1 = ((s8[8388608]{0:T(1024)(128)(4,1)}), s8[4194304]{0:T(1024)(128)(4,1)S(1)}, s32[]{:S(2)}) async-start(s8[8388608]{0:T(1024)(128)(4,1)} %bitcast.177), calls=%async_computation.4 | async-start | bytes 8388608
